TPU v7x, 32 devices: a whole 2x2x4 slice. The times are simulated.
32 devices in a mesh: gx: 4 (over y, x), gy: 4 (over z), ma: 2 (over core).
Axes of the slice: x: 2, y: 2, z: 4, core: 2. Of those that a mesh axis runs over, the one named last changes fastest.
Arguments:
- object_field: float32 [2, 2048, 1536], P(None, 'gx', 'gy'), may hold values from -6 to 6
- probe: float32 [2, 4, 256, 256], P(None, 'ma'), may hold values from -3 to 3
- offsets: int32 [4, 4, 6, 2], P('gx', 'gy'), may hold values from 0 to 511, as said below
- counts: int32 [4, 4], P('gx', 'gy'), may hold values from 1 to 6, as said below
- amplitude: float32 [4, 4, 6, 256, 256], P('gx', 'gy'), may hold values from 0.5 to 3
Outputs:
- object_grad: float32 [2, 2048, 1536], P(None, ('gx', 'ma'), 'gy')
- probe_grad: float32 [2, 4, 256, 256], P(None, 'ma')
Inputs may be any that keep to these rules, and one draw needn't show every extreme that they name: A tile's offsets are below 512 for rows and below 384 for columns; no patch passes the object's last row or column. `counts`: every tile holds at least one live position; in each tile row, tiles v and v + 2 hold at most 8 live positions together; in every draw some tile holds exactly 6 and its partner exactly 2.
All inputs are finite; a program needn't handle non-finite values.
Results may differ from a plain program's by a relative error of at most 0.0003.
Values sent between devices are 32-bit elements; how exact they have to be, the bound alone decides.
A program may use at most 128 MiB of HBM per device.

v0:
```python
import functools

import jax
import jax.numpy as jnp
import ml_dtypes
import numpy as np
from jax import lax
from jax.experimental import pallas as pl
from jax.experimental.pallas import tpu as pltpu
from jax.sharding import PartitionSpec as P

F32 = jnp.float32
BF16 = jnp.bfloat16
MESH = pl.DeviceIdType.MESH
VM = pl.BlockSpec(memory_space=pltpu.VMEM)
ANY = pl.BlockSpec(memory_space=pl.ANY)


def tables(side):
    half = side // 2
    line = np.arange(half)
    found = []
    for odd in (0, 1):
        product = (2 * line[:, None] + odd) * line[None, :] % side
        value = np.exp(-2j * np.pi * product / side) / np.sqrt(side)
        block = np.block([[value.real, -value.imag], [value.imag, value.real]])
        found.append(block)

    def parts(block):
        high = block.astype(np.float32).astype(ml_dtypes.bfloat16)
        low = (block - high.astype(np.float64)).astype(np.float32).astype(ml_dtypes.bfloat16)
        return high, high, low

    tall = [np.concatenate(parts(b), 0) for b in (found[0].T, found[1].T, found[0], found[1])]
    wide = [np.concatenate(parts(b), 1) for b in (found[0], found[1], found[0].T, found[1].T)]
    order = np.concatenate([np.arange(0, side, 2), np.arange(1, side, 2)])
    pick = np.zeros((side, side), np.float32)
    pick[order, np.arange(side)] = 1.0
    picks = np.stack([pick, pick.T]).astype(ml_dtypes.bfloat16)
    return np.stack(tall), np.stack(wide), picks


def split(x):
    high = x.astype(BF16)
    return high, (x - high.astype(F32)).astype(BF16)


def right_mul(x, table):
    high, low = split(x)
    return jnp.dot(jnp.concatenate([high, low, high], 1), table, preferred_element_type=F32)


def left_mul(table, x):
    high, low = split(x)
    return jnp.dot(table, jnp.concatenate([high, low, high], 0), preferred_element_type=F32)


def solve_kernel(off_ref, cnt_ref, core_ref, ext_ref, probe_ref, amp_ref, tall_ref, wide_ref, pick_ref,
                 grad_ref, pg_ref, far_e, far_o):
    step = pl.program_id(0)
    modes, side = probe_ref.shape[1], probe_ref.shape[2]
    half = side // 2
    slot = 2 * step + core_ref[0]

    @pl.when(step == 0)
    def _():
        grad_ref[...] = jnp.zeros_like(grad_ref)
        pg_ref[...] = jnp.zeros_like(pg_ref)

    @pl.when(slot < cnt_ref[0])
    def _():
        row = off_ref[slot, 0]
        col = off_ref[slot, 1]
        base = pl.multiple_of(col // 128 * 128, 128)
        shift = col - base
        width = side + 128
        top_row = pl.multiple_of(row // 8 * 8, 8)
        drop = row - top_row
        tall = side + 8
        window = (pl.ds(top_row, tall), pl.ds(base, width))

        def take(part):
            wide = ext_ref[(part, *window)]
            wide = pltpu.roll(wide, lax.rem(width - shift, width), 1)[:, :side]
            return pltpu.roll(wide, lax.rem(tall - drop, tall), 0)[:side]

        a_re, a_im = take(0), take(1)
        pow_e = pow_o = jnp.zeros((half, side), F32)
        for m in range(modes):
            p_re, p_im = probe_ref[0, m], probe_ref[1, m]
            e_re = p_re * a_re - p_im * a_im
            e_im = p_re * a_im + p_im * a_re
            x_e = jnp.concatenate([e_re[:, :half] + e_re[:, half:], e_im[:, :half] + e_im[:, half:]], 1)
            x_o = jnp.concatenate([e_re[:, :half] - e_re[:, half:], e_im[:, :half] - e_im[:, half:]], 1)
            z_e = right_mul(x_e, tall_ref[0])
            z_o = right_mul(x_o, tall_ref[1])
            z_re = jnp.concatenate([z_e[:, :half], z_o[:, :half]], 1)
            z_im = jnp.concatenate([z_e[:, half:], z_o[:, half:]], 1)
            y_e = jnp.concatenate([z_re[:half] + z_re[half:], z_im[:half] + z_im[half:]], 0)
            y_o = jnp.concatenate([z_re[:half] - z_re[half:], z_im[:half] - z_im[half:]], 0)
            f_e = left_mul(wide_ref[0], y_e)
            f_o = left_mul(wide_ref[1], y_o)
            far_e[m] = f_e
            far_o[m] = f_o
            pow_e = pow_e + (f_e[:half] * f_e[:half] + f_e[half:] * f_e[half:])
            pow_o = pow_o + (f_o[:half] * f_o[:half] + f_o[half:] * f_o[half:])
        measured = jnp.zeros((side, side), F32)
        for term in split(amp_ref[0]):
            moved = jnp.dot(term, pick_ref[0], preferred_element_type=F32).astype(BF16)
            measured = measured + jnp.dot(pick_ref[1], moved, preferred_element_type=F32)
        fac_e = 1.0 - measured[:half] * lax.rsqrt(jnp.maximum(pow_e, 0.25))
        fac_o = 1.0 - measured[half:] * lax.rsqrt(jnp.maximum(pow_o, 0.25))
        fac_e = jnp.concatenate([fac_e, fac_e], 0)
        fac_o = jnp.concatenate([fac_o, fac_o], 0)
        g_re = g_im = jnp.zeros((side, side), F32)
        for m in range(modes):
            q_e = left_mul(wide_ref[2], far_e[m] * fac_e)
            q_o = left_mul(wide_ref[3], far_o[m] * fac_o)
            top, low = q_e + q_o, q_e - q_o
            w_re = jnp.concatenate([top[:half], low[:half]], 0)
            w_im = jnp.concatenate([top[half:], low[half:]], 0)
            s_e = right_mul(jnp.concatenate([w_re[:, :half], w_im[:, :half]], 1), tall_ref[2])
            s_o = right_mul(jnp.concatenate([w_re[:, half:], w_im[:, half:]], 1), tall_ref[3])
            first, second = s_e + s_o, s_e - s_o
            b_re = jnp.concatenate([first[:, :half], second[:, :half]], 1)
            b_im = jnp.concatenate([first[:, half:], second[:, half:]], 1)
            pg_ref[0, m] += a_re * b_re + a_im * b_im
            pg_ref[1, m] += a_re * b_im - a_im * b_re
            p_re, p_im = probe_ref[0, m], probe_ref[1, m]
            g_re = g_re + (p_re * b_re + p_im * b_im)
            g_im = g_im + (p_re * b_im - p_im * b_re)
        for part, value in ((0, g_re), (1, g_im)):
            long = pltpu.roll(jnp.concatenate([value, jnp.zeros((8, side), F32)], 0), drop, 0)
            wide = jnp.concatenate([long, jnp.zeros((tall, 128), F32)], 1)
            grad_ref[(part, *window)] += pltpu.roll(wide, shift, 1)


def remote(src, dst, send, recv, where):
    return pltpu.make_async_remote_copy(src_ref=src, dst_ref=dst, send_sem=send, recv_sem=recv,
                                        device_id=where, device_id_type=MESH)


def greet(barrier, where):
    pl.semaphore_signal(barrier, inc=1, device_id=where, device_id_type=MESH)


def halo_kernel(nx, ny, obj, probe, ext, full, send, recv, own):
    u, v, m = lax.axis_index("gx"), lax.axis_index("gy"), lax.axis_index("ma")
    side = probe.shape[2]
    rows, cols = obj.shape[1], obj.shape[2]
    pm = probe.shape[1]
    other = (u, v, 1 - m)
    keep = [
        pltpu.make_async_copy(obj, ext.at[:, :rows, :cols], own.at[0]),
        pltpu.make_async_copy(probe, full.at[:, pl.ds(m * pm, pm)], own.at[1]),
    ]
    for c in keep:
        c.start()
    links = [
        (v > 0, v < ny - 1, (u, v - 1, m), (u, v + 1, m)),
        (u > 0, u < nx - 1, (u - 1, v, m), (u + 1, v, m)),
        ((u > 0) & (v > 0), (u < nx - 1) & (v < ny - 1), (u - 1, v - 1, m), (u + 1, v + 1, m)),
    ]
    barrier = pltpu.get_barrier_semaphore()
    greet(barrier, other)
    for goes, comes, target, source in links:
        @pl.when(goes)
        def _():
            greet(barrier, target)

        @pl.when(comes)
        def _():
            greet(barrier, source)
    count = lambda flag: jnp.where(flag, 1, 0)
    pl.semaphore_wait(barrier, 1 + sum(count(goes) + count(comes) for goes, comes, _, _ in links))

    def piece(ref, r0, rn, c0, cn):
        return ref.at[m, r0:r0 + rn, c0:c0 + cn]

    h = rows // 2
    pieces = [
        (0, (0, h, 0, side), (0, h, cols, side)),
        (1, (0, side, 0, cols), (rows, side, 0, cols)),
        (0, (h, h, 0, side), (h, h, cols, side)),
        (2, (0, side, 0, side), (rows, side, cols, side)),
    ]
    outs = []
    for n, (link, src, dst) in enumerate(pieces):
        goes, comes, target, source = links[link]
        c = remote(piece(obj, *src), piece(ext, *dst), send.at[n], recv.at[n], target)
        outs.append(c)

        @pl.when(goes)
        def _(c=c):
            c.start()
    mine = pl.ds(m * pm, pm)
    pc = remote(probe, full.at[:, mine], send.at[8], recv.at[8], other)
    pc.start()
    fwds = []
    for n, (link, src, dst) in enumerate(pieces):
        goes, comes, target, source = links[link]
        f = remote(piece(ext, *dst), piece(ext, *dst), send.at[4 + n], recv.at[4 + n], other)
        fwds.append(f)

        @pl.when(comes)
        def _(c=outs[n], f=f):
            c.wait_recv()
            f.start()
    for n, (link, src, dst) in enumerate(pieces):
        goes, comes, target, source = links[link]

        @pl.when(goes)
        def _(c=outs[n]):
            c.wait_send()

        @pl.when(comes)
        def _(f=fwds[n]):
            f.wait()
    pc.wait()
    for c in keep:
        c.wait()


def reduce_kernel(nx, ny, grad, pg, out, pout, rt_r, rt_l, rl, rp, low, edge, r_r, r_b, r_d,
                  acc, rx, px, ry, py, send, recv):
    u, v, m = lax.axis_index("gx"), lax.axis_index("gy"), lax.axis_index("ma")
    side = pg.shape[2]
    rows, cols = out.shape[1], out.shape[2]
    total = rows * 2
    pm = pg.shape[1] // 2
    o = 1 - m
    other = (u, v, o)
    last_x, last_y = nx - 1, ny - 1
    barrier = pltpu.get_barrier_semaphore()
    greet(barrier, other)
    for d in range(1, nx):
        greet(barrier, (lax.rem(u + d, nx), v, m))
        greet(barrier, (lax.rem(u + d, nx), v, o))
    for d in range(1, ny):
        greet(barrier, (u, lax.rem(v + d, ny), m))
    peers = 2 * nx + ny - 2
    corners = [((u < last_x) & (v < last_y), (u + 1, v + 1)), ((u > 0) & (v > 0), (u - 1, v - 1))]
    for there, (a, b) in corners:
        peers = peers + jnp.where(there, 2, 0)

        @pl.when(there)
        def _(a=a, b=b):
            greet(barrier, (a, b, 0))
            greet(barrier, (a, b, 1))
    pl.semaphore_wait(barrier, peers)

    theirs = pl.ds(pl.multiple_of(o * rows, 8), rows)
    mine = pl.ds(pl.multiple_of(m * rows, 8), rows)
    swaps = [
        remote(pg.at[:, pl.ds(o * pm, pm)], rp, send.at[0], recv.at[0], other),
        remote(grad.at[o, total:total + side, :], rl, send.at[1], recv.at[1], other),
        remote(grad.at[:, theirs, cols:cols + side], rt_r, send.at[2], recv.at[2], other),
        remote(grad.at[:, theirs, 0:cols], rt_l, send.at[3], recv.at[3], other),
    ]
    for c in swaps:
        c.start()
    swaps[0].wait_recv()
    for a in range(2):
        for b in range(pm):
            at = (a * pm + b) * side
            acc[at:at + side, :] = pg[a, m * pm + b] + rp[a, b]
    big = acc.shape[0] // nx
    small = big // ny
    gx_rs = []
    for d in range(1, nx):
        to = lax.rem(u + d, nx)
        c = remote(acc.at[pl.ds(pl.multiple_of(to * big, 8), big)], rx.at[d - 1], send.at[7 + d], recv.at[7 + d],
                   (to, v, m))
        c.start()
        gx_rs.append(c)
    swaps[1].wait_recv()
    low[...] = grad[m, total:total + side, :] + rl[...]
    c_b = remote(low.at[:, 0:cols], r_b.at[m], send.at[4], recv.at[4 + m], (u + 1, v, 0))
    c_d = remote(low.at[:, cols:cols + side], r_d.at[m], send.at[5], recv.at[6 + m], (u + 1, v + 1, 0))
    c_r = remote(edge, r_r, send.at[6], recv.at[3 + 5 + 2 * nx], (u, v + 1, m))

    @pl.when(u < last_x)
    def _():
        c_b.start()

    @pl.when((u < last_x) & (v < last_y))
    def _():
        c_d.start()
    swaps[2].wait_recv()
    edge[...] = grad[:, mine, cols:cols + side] + rt_r[...]

    @pl.when(v < last_y)
    def _():
        c_r.start()
    for c in gx_rs:
        c.wait_recv()
    px[...] = acc[pl.ds(pl.multiple_of(u * big, 8), big), :]
    for d in range(1, nx):
        px[...] += rx[d - 1]
    base = 9 + 2 * nx
    gy_rs = []
    for d in range(1, ny):
        to = lax.rem(v + d, ny)
        c = remote(px.at[pl.ds(pl.multiple_of(to * small, 8), small)], ry.at[d - 1], send.at[base + d],
                   recv.at[base + d], (u, to, m))
        c.start()
        gy_rs.append(c)
    swaps[3].wait_recv()
    out[...] = grad[:, mine, 0:cols] + rt_l[...]
    for c in gy_rs:
        c.wait_recv()
    here = pl.ds(pl.multiple_of(u * big + v * small, 8), small)
    part = px[pl.ds(pl.multiple_of(v * small, 8), small), :]
    for d in range(1, ny):
        part = part + ry[d - 1]
    py[...] = part
    pout[here, :] = part
    base = base + ny
    gy_ag = []
    for d in range(1, ny):
        to = lax.rem(v + d, ny)
        c = remote(py, pout.at[here], send.at[base + d], recv.at[base + d], (u, to, m))
        c.start()
        gy_ag.append(c)
    for c in gy_ag:
        c.wait_recv()
    band = pl.ds(pl.multiple_of(u * big, 8), big)
    gx_ag = []
    for d in range(1, nx):
        to = lax.rem(u + d, nx)
        c = remote(pout.at[band], pout.at[band], send.at[7 + nx + d], recv.at[7 + nx + d], (to, v, m))
        c.start()
        gx_ag.append(c)

    @pl.when(v > 0)
    def _():
        c_r.wait_recv()
        out[:, :, 0:side] += r_r[...]

    @pl.when((u > 0) & (m == 0))
    def _():
        for k in range(2):
            remote(low.at[:, 0:cols], r_b.at[k], send.at[4], recv.at[4 + k], other).wait_recv()
        out[:, 0:side, :] += r_b[...]

    @pl.when((u > 0) & (v > 0) & (m == 0))
    def _():
        for k in range(2):
            remote(low.at[:, cols:cols + side], r_d.at[k], send.at[5], recv.at[6 + k], other).wait_recv()
        out[:, 0:side, 0:side] += r_d[...]
    for c in gx_ag:
        c.wait_recv()
    for c in swaps + gx_rs + gy_rs + gy_ag + gx_ag:
        c.wait_send()

    @pl.when(u < last_x)
    def _():
        c_b.wait_send()

    @pl.when((u < last_x) & (v < last_y))
    def _():
        c_d.wait_send()

    @pl.when(v < last_y)
    def _():
        c_r.wait_send()


def local(nx, ny, object_field, probe, offsets, counts, amplitude):
    side = probe.shape[2]
    own_modes = probe.shape[1]
    modes = own_modes * 2
    rows, cols = object_field.shape[1:]
    cap = offsets.shape[2]
    dma = pltpu.SemaphoreType.DMA
    ext, full = pl.pallas_call(
        functools.partial(halo_kernel, nx, ny),
        name="halo",
        out_shape=(jax.ShapeDtypeStruct((2, rows + side, cols + side), F32),
                   jax.ShapeDtypeStruct((2, modes, side, side), F32)),
        in_specs=[ANY, ANY],
        out_specs=(ANY, ANY),
        scratch_shapes=[dma((9,)), dma((9,)), dma((2,))],
        compiler_params=pltpu.CompilerParams(collective_id=0, has_side_effects=True),
    )(object_field, probe)
    tall, wide, picks = tables(side)
    core = lax.axis_index("ma").astype(jnp.int32).reshape(1)
    whole = lambda shape: pl.BlockSpec(shape, lambda i, *_: (0,) * len(shape), pipeline_mode=pl.Buffered(1))
    grad, pg = pl.pallas_call(
        solve_kernel,
        name="solve",
        out_shape=(jax.ShapeDtypeStruct(ext.shape, F32), jax.ShapeDtypeStruct(full.shape, F32)),
        grid_spec=pltpu.PrefetchScalarGridSpec(
            num_scalar_prefetch=3,
            grid=(cap // 2,),
            in_specs=[
                whole(ext.shape), whole(full.shape),
                pl.BlockSpec((1, side, side), lambda i, off, cnt, core: (2 * i + core[0], 0, 0)),
                whole(tall.shape), whole(wide.shape), whole(picks.shape),
            ],
            out_specs=(whole(ext.shape), whole(full.shape)),
            scratch_shapes=[pltpu.VMEM((modes, side, side), F32), pltpu.VMEM((modes, side, side), F32)],
        ),
        compiler_params=pltpu.CompilerParams(vmem_limit_bytes=48 << 20),
    )(offsets[0, 0], counts[0], core, ext, full, amplitude[0, 0],
      jnp.asarray(tall), jnp.asarray(wide), jnp.asarray(picks))
    half = rows // 2
    flat = 2 * own_modes * side
    big = flat // nx
    nsem = 9 + 2 * nx + 2 * ny + 2
    object_grad, probe_grad = pl.pallas_call(
        functools.partial(reduce_kernel, nx, ny),
        name="reduce",
        out_shape=(jax.ShapeDtypeStruct((2, half, cols), F32), jax.ShapeDtypeStruct((flat, side), F32)),
        in_specs=[VM, VM],
        out_specs=(VM, VM),
        scratch_shapes=[
            pltpu.VMEM((2, half, side), F32), pltpu.VMEM((2, half, cols), F32),
            pltpu.VMEM((side, cols + side), F32), pltpu.VMEM((2, own_modes, side, side), F32),
            pltpu.VMEM((side, cols + side), F32), pltpu.VMEM((2, half, side), F32),
            pltpu.VMEM((2, half, side), F32), pltpu.VMEM((2, side, cols), F32), pltpu.VMEM((2, side, side), F32),
            pltpu.VMEM((flat, side), F32), pltpu.VMEM((nx - 1, big, side), F32), pltpu.VMEM((big, side), F32),
            pltpu.VMEM((ny - 1, big // ny, side), F32), pltpu.VMEM((big // ny, side), F32),
            dma((nsem,)), dma((nsem,)),
        ],
        compiler_params=pltpu.CompilerParams(collective_id=1, has_side_effects=True, vmem_limit_bytes=48 << 20),
    )(grad, pg)
    return object_grad, probe_grad.reshape(2, own_modes, side, side)


def solution(mesh):
    return jax.shard_map(
        functools.partial(local, mesh.shape["gx"], mesh.shape["gy"]),
        mesh=mesh,
        in_specs=(
            P(None, "gx", "gy"),
            P(None, "ma", None, None),
            P("gx", "gy", None, None),
            P("gx", "gy"),
            P("gx", "gy", None, None, None),
        ),
        out_specs=(P(None, ("gx", "ma"), "gy"), P(None, "ma", None, None)),
        check_vma=False,
    )
```

profile of v0, /device:TPU:0, one launch (start us, length us, event | category | flops | bytes accessed | tf_op | source)
XLA Modules:
  0.0 168.6 jit_solution(17219782407839685464)
XLA Ops:
  0.6 0.0 copy-start.4
  0.6 0.0 copy-start.1
  1.4 0.8 copy.10.off_ref
  2.2 80.7 %halo.1 = (f32[2,768,640]{2,1,0:T(8,128)}, f32[2,4,256,256]{3,2,1,0:T(8,128)}) custom-call(f32[2,512,384]{2,1,0:T(8,128)} %obj.1, f32[2,2,256,256]{3,2,1,0:T(8,128)} %probe.1), custom_call_target="tpu_custom_call" | custom-call | tf_op jit(solution)/shard_map/halo/pallas_call | solution.py:376
  82.9 0.0 copy-done.4
  82.9 0.0 copy-done.1
  82.9 0.0 copy-start.2
  82.9 1.4 copy-done.2
  84.3 0.0 copy-start.3
  84.3 1.4 copy-done.3
  85.7 19.7 %solve.1 = (f32[2,768,640]{2,1,0:T(8,128)}, f32[2,4,256,256]{3,2,1,0:T(8,128)}) custom-call(s32[6,2]{1,0:T(8,128)S(1)} %copy.10.off_ref, s32[1]{0:T(128)} %bitcast.5.cnt_ref, s32[1]{0:T(128)} %bitcast.2.core_ref, f32[2,768,640]{2,1,0:T(8,128)} %get-tuple-element.8.ext_ref, f32[2,4,256,256]{3,2,1,0:T(8,128)} %get-tuple-element.9.probe_ref, ...), custom_call_target="tpu_custom_call" | custom-call | tf_op jit(solution)/shard_map/solve/pallas_call | solution.py:389
  105.4 0.0 copy-start
  105.4 1.6 copy-done
  107.0 59.7 %reduce.1 = (f32[2,256,384]{2,1,0:T(8,128)S(1)}, f32[1024,256]{1,0:T(8,128)S(1)}) custom-call(f32[2,768,640]{2,1,0:T(8,128)} %get-tuple-element.10.grad, f32[2,4,256,256]{3,2,1,0:T(8,128)S(1)} %copy-done), custom_call_target="tpu_custom_call" | custom-call | tf_op jit(solution)/shard_map/reduce/pallas_call | solution.py:411
  166.8 0.9 copy.14
  167.6 1.0 copy.15
Async XLA Ops:
  0.6 82.3 %copy-start.4 = (bf16[2,256,256]{2,1,0:T(8,128)(2,1)S(1)}, bf16[2,256,256]{2,1,0:T(8,128)(2,1)}, u32[]{:S(2)}) copy-start(bf16[2,256,256]{2,1,0:T(8,128)(2,1)} %constant.12.clone.pick_ref) | copy-start | bytes 786436
  0.6 82.3 %copy-start.1 = (f32[1,1,6,256,256]{4,3,2,1,0:T(8,128)S(1)}, f32[1,1,6,256,256]{4,3,2,1,0:T(8,128)}, u32[]{:S(2)}) copy-start(f32[1,1,6,256,256]{4,3,2,1,0:T(8,128)} %param.12) | copy-start | bytes 4718596
  82.9 1.4 copy-start.2
  84.3 1.4 copy-start.3
  105.4 1.6 copy-start
where the time goes:
time: 169 us
  Pallas kernels  160 us (95%)
  local copies, waits for them, and re-layouts  7.03 us (4%)
    pallas_call x1, Pallas kernels, local(): pl.pallas_call(functools.partial(halo_kernel, nx, ny), name='halo', out_s...  80.7 us
    pallas_call x1, Pallas kernels, local(): pl.pallas_call(functools.partial(reduce_kernel, nx, ny), name='reduce', o...  59.7 us
    pallas_call x1, Pallas kernels, local(): pl.pallas_call(solve_kernel, name='solve', out_shape=(jax.ShapeDtypeStruc...  19.7 us
    unnamed x12, local copies, waits for them, and re-layouts  6.26 us

commit v1 on v0

--- a/solution.py
+++ b/solution.py
@@ -13,7 +13,6 @@
 BF16 = jnp.bfloat16
 MESH = pl.DeviceIdType.MESH
 VM = pl.BlockSpec(memory_space=pltpu.VMEM)
-ANY = pl.BlockSpec(memory_space=pl.ANY)
 
 
 def tables(side):
@@ -144,81 +143,69 @@
     pl.semaphore_signal(barrier, inc=1, device_id=where, device_id_type=MESH)
 
 
-def halo_kernel(nx, ny, obj, probe, ext, full, send, recv, own):
+def halo_kernel(nx, ny, obj, probe, ext, full, send, recv):
     u, v, m = lax.axis_index("gx"), lax.axis_index("gy"), lax.axis_index("ma")
     side = probe.shape[2]
     rows, cols = obj.shape[1], obj.shape[2]
     pm = probe.shape[1]
     other = (u, v, 1 - m)
-    keep = [
-        pltpu.make_async_copy(obj, ext.at[:, :rows, :cols], own.at[0]),
-        pltpu.make_async_copy(probe, full.at[:, pl.ds(m * pm, pm)], own.at[1]),
-    ]
-    for c in keep:
-        c.start()
-    links = [
-        (v > 0, v < ny - 1, (u, v - 1, m), (u, v + 1, m)),
-        (u > 0, u < nx - 1, (u - 1, v, m), (u + 1, v, m)),
-        ((u > 0) & (v > 0), (u < nx - 1) & (v < ny - 1), (u - 1, v - 1, m), (u + 1, v + 1, m)),
-    ]
+    right, below = v < ny - 1, u < nx - 1
+    left_dev, right_dev = (u, v - 1, m), (u, v + 1, m)
+    up_dev, down_dev = (u - 1, v, m), (u + 1, v, m)
     barrier = pltpu.get_barrier_semaphore()
     greet(barrier, other)
-    for goes, comes, target, source in links:
-        @pl.when(goes)
-        def _():
-            greet(barrier, target)
-
-        @pl.when(comes)
-        def _():
-            greet(barrier, source)
-    count = lambda flag: jnp.where(flag, 1, 0)
-    pl.semaphore_wait(barrier, 1 + sum(count(goes) + count(comes) for goes, comes, _, _ in links))
+    peers = 1
+    for there, where in ((v > 0, left_dev), (right, right_dev), (u > 0, up_dev), (below, down_dev)):
+        peers = peers + jnp.where(there, 1, 0)
+
+        @pl.when(there)
+        def _(where=where):
+            greet(barrier, where)
+    pl.semaphore_wait(barrier, peers)
 
     def piece(ref, r0, rn, c0, cn):
         return ref.at[m, r0:r0 + rn, c0:c0 + cn]
 
-    h = rows // 2
-    pieces = [
-        (0, (0, h, 0, side), (0, h, cols, side)),
-        (1, (0, side, 0, cols), (rows, side, 0, cols)),
-        (0, (h, h, 0, side), (h, h, cols, side)),
-        (2, (0, side, 0, side), (rows, side, cols, side)),
+    h = rows - side
+    first, rest = (0, side, cols, side), (side, h, cols, side)
+    under, corner = (rows, side, 0, cols), (rows, side, cols, side)
+    hops = [
+        (piece(obj, 0, side, 0, side), first, v > 0, right, left_dev),
+        (piece(obj, 0, side, 0, cols), under, u > 0, below, up_dev),
+        (piece(obj, side, h, 0, side), rest, v > 0, right, left_dev),
+        (piece(ext, *first), corner, (u > 0) & right, below & right, up_dev),
     ]
-    outs = []
-    for n, (link, src, dst) in enumerate(pieces):
-        goes, comes, target, source = links[link]
-        c = remote(piece(obj, *src), piece(ext, *dst), send.at[n], recv.at[n], target)
-        outs.append(c)
-
-        @pl.when(goes)
-        def _(c=c):
-            c.start()
+    outs, fwds = [], []
+    for n, (src, place, goes, comes, target) in enumerate(hops):
+        outs.append(remote(src, piece(ext, *place), send.at[n], recv.at[n], target))
+        fwds.append(remote(piece(ext, *place), piece(ext, *place), send.at[4 + n], recv.at[4 + n], other))
+    for n in range(3):
+        @pl.when(hops[n][2])
+        def _(n=n):
+            outs[n].start()
     mine = pl.ds(m * pm, pm)
     pc = remote(probe, full.at[:, mine], send.at[8], recv.at[8], other)
     pc.start()
-    fwds = []
-    for n, (link, src, dst) in enumerate(pieces):
-        goes, comes, target, source = links[link]
-        f = remote(piece(ext, *dst), piece(ext, *dst), send.at[4 + n], recv.at[4 + n], other)
-        fwds.append(f)
-
+    ext[:, 0:rows, 0:cols] = obj[...]
+    full[:, mine] = probe[...]
+    for n, (src, place, goes, comes, target) in enumerate(hops):
         @pl.when(comes)
-        def _(c=outs[n], f=f):
-            c.wait_recv()
-            f.start()
-    for n, (link, src, dst) in enumerate(pieces):
-        goes, comes, target, source = links[link]
-
+        def _(n=n):
+            outs[n].wait_recv()
+            if n == 0:
+                @pl.when(u > 0)
+                def _():
+                    outs[3].start()
+            fwds[n].start()
+    for n, (src, place, goes, comes, target) in enumerate(hops):
         @pl.when(goes)
-        def _(c=outs[n]):
-            c.wait_send()
+        def _(n=n):
+            outs[n].wait_send()
 
         @pl.when(comes)
-        def _(f=fwds[n]):
-            f.wait()
+        def _(n=n):
+            fwds[n].wait()
     pc.wait()
-    for c in keep:
-        c.wait()
 
 
 def reduce_kernel(nx, ny, grad, pg, out, pout, rt_r, rt_l, rl, rp, low, edge, r_r, r_b, r_d,
@@ -239,14 +226,6 @@
     for d in range(1, ny):
         greet(barrier, (u, lax.rem(v + d, ny), m))
     peers = 2 * nx + ny - 2
-    corners = [((u < last_x) & (v < last_y), (u + 1, v + 1)), ((u > 0) & (v > 0), (u - 1, v - 1))]
-    for there, (a, b) in corners:
-        peers = peers + jnp.where(there, 2, 0)
-
-        @pl.when(there)
-        def _(a=a, b=b):
-            greet(barrier, (a, b, 0))
-            greet(barrier, (a, b, 1))
     pl.semaphore_wait(barrier, peers)
 
     theirs = pl.ds(pl.multiple_of(o * rows, 8), rows)
@@ -275,17 +254,9 @@
         gx_rs.append(c)
     swaps[1].wait_recv()
     low[...] = grad[m, total:total + side, :] + rl[...]
-    c_b = remote(low.at[:, 0:cols], r_b.at[m], send.at[4], recv.at[4 + m], (u + 1, v, 0))
-    c_d = remote(low.at[:, cols:cols + side], r_d.at[m], send.at[5], recv.at[6 + m], (u + 1, v + 1, 0))
+    c_b = remote(low, r_b.at[m], send.at[4], recv.at[4 + m], (u + 1, v, 0))
+    c_d = remote(r_b.at[:, :, cols:cols + side], r_d, send.at[5], recv.at[6], (u, v + 1, 0))
     c_r = remote(edge, r_r, send.at[6], recv.at[3 + 5 + 2 * nx], (u, v + 1, m))
-
-    @pl.when(u < last_x)
-    def _():
-        c_b.start()
-
-    @pl.when((u < last_x) & (v < last_y))
-    def _():
-        c_d.start()
     swaps[2].wait_recv()
     edge[...] = grad[:, mine, cols:cols + side] + rt_r[...]
 
@@ -294,6 +265,10 @@
         c_r.start()
     for c in gx_rs:
         c.wait_recv()
+
+    @pl.when(u < last_x)
+    def _():
+        c_b.start()
     px[...] = acc[pl.ds(pl.multiple_of(u * big, 8), big), :]
     for d in range(1, nx):
         px[...] += rx[d - 1]
@@ -340,14 +315,17 @@
     @pl.when((u > 0) & (m == 0))
     def _():
         for k in range(2):
-            remote(low.at[:, 0:cols], r_b.at[k], send.at[4], recv.at[4 + k], other).wait_recv()
-        out[:, 0:side, :] += r_b[...]
-
-    @pl.when((u > 0) & (v > 0) & (m == 0))
-    def _():
-        for k in range(2):
-            remote(low.at[:, cols:cols + side], r_d.at[k], send.at[5], recv.at[6 + k], other).wait_recv()
-        out[:, 0:side, 0:side] += r_d[...]
+            remote(low, r_b.at[k], send.at[4], recv.at[4 + k], other).wait_recv()
+
+        @pl.when(v < last_y)
+        def _():
+            c_d.start()
+        out[:, 0:side, :] += r_b[:, :, 0:cols]
+
+        @pl.when(v > 0)
+        def _():
+            c_d.wait_recv()
+            out[:, 0:side, 0:side] += r_d[...]
     for c in gx_ag:
         c.wait_recv()
     for c in swaps + gx_rs + gy_rs + gy_ag + gx_ag:
@@ -357,7 +335,7 @@
     def _():
         c_b.wait_send()
 
-    @pl.when((u < last_x) & (v < last_y))
+    @pl.when((u > 0) & (v < last_y) & (m == 0))
     def _():
         c_d.wait_send()
 
@@ -378,10 +356,10 @@
         name="halo",
         out_shape=(jax.ShapeDtypeStruct((2, rows + side, cols + side), F32),
                    jax.ShapeDtypeStruct((2, modes, side, side), F32)),
-        in_specs=[ANY, ANY],
-        out_specs=(ANY, ANY),
-        scratch_shapes=[dma((9,)), dma((9,)), dma((2,))],
-        compiler_params=pltpu.CompilerParams(collective_id=0, has_side_effects=True),
+        in_specs=[VM, VM],
+        out_specs=(VM, VM),
+        scratch_shapes=[dma((9,)), dma((9,))],
+        compiler_params=pltpu.CompilerParams(collective_id=0, has_side_effects=True, vmem_limit_bytes=48 << 20),
     )(object_field, probe)
     tall, wide, picks = tables(side)
     core = lax.axis_index("ma").astype(jnp.int32).reshape(1)
@@ -418,7 +396,7 @@
             pltpu.VMEM((2, half, side), F32), pltpu.VMEM((2, half, cols), F32),
             pltpu.VMEM((side, cols + side), F32), pltpu.VMEM((2, own_modes, side, side), F32),
             pltpu.VMEM((side, cols + side), F32), pltpu.VMEM((2, half, side), F32),
-            pltpu.VMEM((2, half, side), F32), pltpu.VMEM((2, side, cols), F32), pltpu.VMEM((2, side, side), F32),
+            pltpu.VMEM((2, half, side), F32), pltpu.VMEM((2, side, cols + side), F32), pltpu.VMEM((2, side, side), F32),
             pltpu.VMEM((flat, side), F32), pltpu.VMEM((nx - 1, big, side), F32), pltpu.VMEM((big, side), F32),
             pltpu.VMEM((ny - 1, big // ny, side), F32), pltpu.VMEM((big // ny, side), F32),
             dma((nsem,)), dma((nsem,)),

time: 169 us -> 108 us (0.64)
  Pallas kernels: 160 us -> 95.4 us
  local copies, waits for them, and re-layouts: 7.03 us -> 11 us
    pallas_call x1, Pallas kernels: 80.7 us -> 22.2 us  [local(): pl.pallas_call(functools.partial(halo_kernel, nx, ny), name='halo', out_s...]
    pallas_call x1, Pallas kernels: 59.7 us -> 46.9 us  [local(): pl.pallas_call(functools.partial(reduce_kernel, nx, ny), name='reduce', o...]
    pallas_call x1, Pallas kernels: 19.7 us -> 26.4 us  [local(): pl.pallas_call(solve_kernel, name='solve', out_shape=(jax.ShapeDtypeStruc...]
    unnamed x12 -> x18, local copies, waits for them, and re-layouts: 6.26 us -> 10.3 us
where the time goes in v1:
time: 108 us
  Pallas kernels  95.4 us (88%)
  local copies, waits for them, and re-layouts  11 us (10%)
  between operations  1.31 us (1%)
    pallas_call x1, Pallas kernels, local(): pl.pallas_call(functools.partial(reduce_kernel, nx, ny), name='reduce', o...  46.9 us
    pallas_call x1, Pallas kernels, local(): pl.pallas_call(solve_kernel, name='solve', out_shape=(jax.ShapeDtypeStruc...  26.4 us
    pallas_call x1, Pallas kernels, local(): pl.pallas_call(functools.partial(halo_kernel, nx, ny), name='halo', out_s...  22.2 us
    unnamed x18, local copies, waits for them, and re-layouts  10.3 us

profile of v1, /device:TPU:0, one launch (start us, length us, event | category | flops | bytes accessed | tf_op | source)
XLA Modules:
  0.0 107.8 jit_solution(1946218638307703242)
XLA Ops:
  1.3 0.8 copy.10.off_ref
  2.0 0.0 copy-start.2
  2.0 1.4 %copy-done.2 = f32[2,512,384]{2,1,0:T(8,128)S(1)} copy-done((f32[2,512,384]{2,1,0:T(8,128)S(1)}, f32[2,512,384]{2,1,0:T(8,128)}, u32[]{:S(2)}) %copy-start.2) | copy-done | bytes 1572888
  3.5 0.0 copy-start.6
  3.5 1.2 %copy-done.6 = f32[2,2,256,256]{3,2,1,0:T(8,128)S(1)} copy-done((f32[2,2,256,256]{3,2,1,0:T(8,128)S(1)}, f32[2,2,256,256]{3,2,1,0:T(8,128)}, u32[]{:S(2)}) %copy-start.6) | copy-done | bytes 1048600
  4.7 0.0 copy-start.3
  4.7 0.0 copy-start.7
  4.7 22.2 %halo.1 = (f32[2,768,640]{2,1,0:T(8,128)}, f32[2,4,256,256]{3,2,1,0:T(8,128)S(1)}) custom-call(f32[2,512,384]{2,1,0:T(8,128)S(1)} %copy-done.2, f32[2,2,256,256]{3,2,1,0:T(8,128)S(1)} %copy-done.6), custom_call_target="tpu_custom_call" | custom-call | tf_op jit(solution)/shard_map/halo/pallas_call | solution.py:354
  26.9 0.0 copy-start.1
  26.9 1.4 %copy-done.1 = f32[2,4,256,256]{3,2,1,0:T(8,128)} copy-done((f32[2,4,256,256]{3,2,1,0:T(8,128)}, f32[2,4,256,256]{3,2,1,0:T(8,128)S(1)}, u32[]{:S(2)}) %copy-start.1) | copy-done | bytes 2097176
  28.2 0.0 copy-done.3
  28.2 0.0 copy-done.7
  28.2 0.0 copy-start.4
  28.2 1.4 %copy-done.4 = bf16[4,256,768]{2,1,0:T(8,128)(2,1)S(1)} copy-done((bf16[4,256,768]{2,1,0:T(8,128)(2,1)S(1)}, bf16[4,256,768]{2,1,0:T(8,128)(2,1)}, u32[]{:S(2)}) %copy-start.4) | copy-done | bytes 1572888
  29.6 0.0 copy-start.5
  29.6 1.4 %copy-done.5 = bf16[4,768,256]{2,1,0:T(8,128)(2,1)S(1)} copy-done((bf16[4,768,256]{2,1,0:T(8,128)(2,1)S(1)}, bf16[4,768,256]{2,1,0:T(8,128)(2,1)}, u32[]{:S(2)}) %copy-start.5) | copy-done | bytes 1572888
  31.1 26.4 %solve.1 = (f32[2,768,640]{2,1,0:T(8,128)}, f32[2,4,256,256]{3,2,1,0:T(8,128)}) custom-call(s32[6,2]{1,0:T(8,128)S(1)} %copy.10.off_ref, s32[1]{0:T(128)} %bitcast.5.cnt_ref, s32[1]{0:T(128)} %bitcast.2.core_ref, f32[2,768,640]{2,1,0:T(8,128)} %get-tuple-element.8.ext_ref, f32[2,4,256,256]{3,2,1,0:T(8,128)} %copy-done.1, f32[6,256,256]{2,1,0:T(8,128)S(1)} %bitcast.6, ...), custom_call_target="tpu_custom_call" | custom-call | tf_op jit(solution)/shard_map/solve/pallas_call | solution.py:367
  57.4 0.0 copy-start
  57.4 1.6 %copy-done = f32[2,4,256,256]{3,2,1,0:T(8,128)S(1)} copy-done((f32[2,4,256,256]{3,2,1,0:T(8,128)S(1)}, f32[2,4,256,256]{3,2,1,0:T(8,128)}, u32[]{:S(2)}) %copy-start) | copy-done | bytes 2097176
  59.0 46.9 %reduce.1 = (f32[2,256,384]{2,1,0:T(8,128)S(1)}, f32[1024,256]{1,0:T(8,128)S(1)}) custom-call(f32[2,768,640]{2,1,0:T(8,128)} %get-tuple-element.10.grad, f32[2,4,256,256]{3,2,1,0:T(8,128)S(1)} %copy-done), custom_call_target="tpu_custom_call" | custom-call | tf_op jit(solution)/shard_map/reduce/pallas_call | solution.py:389
  105.9 0.9 copy.14
  106.8 1.0 copy.15
Async XLA Ops:
  2.0 1.4 %copy-start.2 = (f32[2,512,384]{2,1,0:T(8,128)S(1)}, f32[2,512,384]{2,1,0:T(8,128)}, u32[]{:S(2)}) copy-start(f32[2,512,384]{2,1,0:T(8,128)} %obj.1) | copy-start | bytes 4718596
  3.5 1.2 %copy-start.6 = (f32[2,2,256,256]{3,2,1,0:T(8,128)S(1)}, f32[2,2,256,256]{3,2,1,0:T(8,128)}, u32[]{:S(2)}) copy-start(f32[2,2,256,256]{3,2,1,0:T(8,128)} %probe.1) | copy-start | bytes 3145732
  4.7 23.6 %copy-start.3 = (f32[1,1,6,256,256]{4,3,2,1,0:T(8,128)S(1)}, f32[1,1,6,256,256]{4,3,2,1,0:T(8,128)}, u32[]{:S(2)}) copy-start(f32[1,1,6,256,256]{4,3,2,1,0:T(8,128)} %param.12) | copy-start | bytes 4718596
  4.7 23.6 %copy-start.7 = (bf16[2,256,256]{2,1,0:T(8,128)(2,1)S(1)}, bf16[2,256,256]{2,1,0:T(8,128)(2,1)}, u32[]{:S(2)}) copy-start(bf16[2,256,256]{2,1,0:T(8,128)(2,1)} %constant.12.clone.pick_ref) | copy-start | bytes 786436
  26.9 1.4 %copy-start.1 = (f32[2,4,256,256]{3,2,1,0:T(8,128)}, f32[2,4,256,256]{3,2,1,0:T(8,128)S(1)}, u32[]{:S(2)}) copy-start(f32[2,4,256,256]{3,2,1,0:T(8,128)S(1)} %get-tuple-element.9.probe_ref) | copy-start | bytes 6291460
  28.2 1.4 %copy-start.4 = (bf16[4,256,768]{2,1,0:T(8,128)(2,1)S(1)}, bf16[4,256,768]{2,1,0:T(8,128)(2,1)}, u32[]{:S(2)}) copy-start(bf16[4,256,768]{2,1,0:T(8,128)(2,1)} %constant.11.clone.wide_ref) | copy-start | bytes 4718596
  29.6 1.4 %copy-start.5 = (bf16[4,768,256]{2,1,0:T(8,128)(2,1)S(1)}, bf16[4,768,256]{2,1,0:T(8,128)(2,1)}, u32[]{:S(2)}) copy-start(bf16[4,768,256]{2,1,0:T(8,128)(2,1)} %constant.10.clone.tall_ref) | copy-start | bytes 4718596
  57.4 1.6 %copy-start = (f32[2,4,256,256]{3,2,1,0:T(8,128)S(1)}, f32[2,4,256,256]{3,2,1,0:T(8,128)}, u32[]{:S(2)}) copy-start(f32[2,4,256,256]{3,2,1,0:T(8,128)} %get-tuple-element.11.pg) | copy-start | bytes 6291460

commit v2 on v1

--- a/solution.py
+++ b/solution.py
@@ -12,6 +12,7 @@
 F32 = jnp.float32
 BF16 = jnp.bfloat16
 MESH = pl.DeviceIdType.MESH
+SM = pl.BlockSpec(memory_space=pltpu.SMEM)
 VM = pl.BlockSpec(memory_space=pltpu.VMEM)
 
 
@@ -56,18 +57,14 @@
 
 def solve_kernel(off_ref, cnt_ref, core_ref, ext_ref, probe_ref, amp_ref, tall_ref, wide_ref, pick_ref,
                  grad_ref, pg_ref, far_e, far_o):
-    step = pl.program_id(0)
     modes, side = probe_ref.shape[1], probe_ref.shape[2]
     half = side // 2
-    slot = 2 * step + core_ref[0]
-
-    @pl.when(step == 0)
-    def _():
-        grad_ref[...] = jnp.zeros_like(grad_ref)
-        pg_ref[...] = jnp.zeros_like(pg_ref)
-
-    @pl.when(slot < cnt_ref[0])
-    def _():
+    grad_ref[...] = jnp.zeros_like(grad_ref)
+    pg_ref[...] = jnp.zeros_like(pg_ref)
+
+    @pl.loop(0, (cnt_ref[0] + 1 - core_ref[0]) // 2)
+    def _(step):
+        slot = 2 * step + core_ref[0]
         row = off_ref[slot, 0]
         col = off_ref[slot, 1]
         base = pl.multiple_of(col // 128 * 128, 128)
@@ -104,7 +101,7 @@
             pow_e = pow_e + (f_e[:half] * f_e[:half] + f_e[half:] * f_e[half:])
             pow_o = pow_o + (f_o[:half] * f_o[:half] + f_o[half:] * f_o[half:])
         measured = jnp.zeros((side, side), F32)
-        for term in split(amp_ref[0]):
+        for term in split(amp_ref[slot]):
             moved = jnp.dot(term, pick_ref[0], preferred_element_type=F32).astype(BF16)
             measured = measured + jnp.dot(pick_ref[1], moved, preferred_element_type=F32)
         fac_e = 1.0 - measured[:half] * lax.rsqrt(jnp.maximum(pow_e, 0.25))
@@ -359,27 +356,19 @@
         in_specs=[VM, VM],
         out_specs=(VM, VM),
         scratch_shapes=[dma((9,)), dma((9,))],
-        compiler_params=pltpu.CompilerParams(collective_id=0, has_side_effects=True, vmem_limit_bytes=48 << 20),
+        cost_estimate=pl.CostEstimate(flops=0, transcendentals=0, bytes_accessed=64 << 20),
+        compiler_params=pltpu.CompilerParams(collective_id=0, has_side_effects=True, vmem_limit_bytes=12 << 20),
     )(object_field, probe)
     tall, wide, picks = tables(side)
     core = lax.axis_index("ma").astype(jnp.int32).reshape(1)
-    whole = lambda shape: pl.BlockSpec(shape, lambda i, *_: (0,) * len(shape), pipeline_mode=pl.Buffered(1))
     grad, pg = pl.pallas_call(
         solve_kernel,
         name="solve",
         out_shape=(jax.ShapeDtypeStruct(ext.shape, F32), jax.ShapeDtypeStruct(full.shape, F32)),
-        grid_spec=pltpu.PrefetchScalarGridSpec(
-            num_scalar_prefetch=3,
-            grid=(cap // 2,),
-            in_specs=[
-                whole(ext.shape), whole(full.shape),
-                pl.BlockSpec((1, side, side), lambda i, off, cnt, core: (2 * i + core[0], 0, 0)),
-                whole(tall.shape), whole(wide.shape), whole(picks.shape),
-            ],
-            out_specs=(whole(ext.shape), whole(full.shape)),
-            scratch_shapes=[pltpu.VMEM((modes, side, side), F32), pltpu.VMEM((modes, side, side), F32)],
-        ),
-        compiler_params=pltpu.CompilerParams(vmem_limit_bytes=48 << 20),
+        in_specs=[SM, SM, SM] + [VM] * 6,
+        out_specs=(VM, VM),
+        scratch_shapes=[pltpu.VMEM((modes, side, side), F32), pltpu.VMEM((modes, side, side), F32)],
+        compiler_params=pltpu.CompilerParams(vmem_limit_bytes=24 << 20),
     )(offsets[0, 0], counts[0], core, ext, full, amplitude[0, 0],
       jnp.asarray(tall), jnp.asarray(wide), jnp.asarray(picks))
     half = rows // 2
@@ -401,7 +390,7 @@
             pltpu.VMEM((ny - 1, big // ny, side), F32), pltpu.VMEM((big // ny, side), F32),
             dma((nsem,)), dma((nsem,)),
         ],
-        compiler_params=pltpu.CompilerParams(collective_id=1, has_side_effects=True, vmem_limit_bytes=48 << 20),
+        compiler_params=pltpu.CompilerParams(collective_id=1, has_side_effects=True, vmem_limit_bytes=18 << 20),
     )(grad, pg)
     return object_grad, probe_grad.reshape(2, own_modes, side, side)
 

time: 108 us -> 97 us (0.90)
  Pallas kernels: 95.4 us -> 87.4 us
  local copies, waits for them, and re-layouts: 11 us -> 8.07 us
    pallas_call x1, Pallas kernels: 26.4 us -> 7.67 us  [local(): pl.pallas_call(solve_kernel, name='solve', out_shape=(jax.ShapeDtypeStruc...]
    pallas_call x1, Pallas kernels: 46.9 us -> 59.5 us  [local(): pl.pallas_call(functools.partial(reduce_kernel, nx, ny), name='reduce', o...]
    unnamed x18 -> x14, local copies, waits for them, and re-layouts: 10.3 us -> 7.3 us
    pallas_call x1, Pallas kernels: 22.2 us -> 20.3 us  [local(): pl.pallas_call(functools.partial(halo_kernel, nx, ny), name='halo', out_s...]
where the time goes in v2:
time: 97 us; the launch traced here: 96.8 us
  Pallas kernels  87.4 us (90%)
  local copies, waits for them, and re-layouts  8.07 us (8%)
  between operations  1.33 us (1%)
    pallas_call x1, Pallas kernels, local(): pl.pallas_call(functools.partial(reduce_kernel, nx, ny), name='reduce', o...  59.5 us
    pallas_call x1, Pallas kernels, local(): pl.pallas_call(functools.partial(halo_kernel, nx, ny), name='halo', out_s...  20.3 us
    pallas_call x1, Pallas kernels, local(): pl.pallas_call(solve_kernel, name='solve', out_shape=(jax.ShapeDtypeStruc...  7.67 us
    unnamed x14, local copies, waits for them, and re-layouts  7.3 us

profile of v2, /device:TPU:0, one launch (start us, length us, event | category | flops | bytes accessed | tf_op | source)
XLA Modules:
  0.0 96.8 jit_solution(16362274341336706564)
XLA Ops:
  1.3 0.8 copy.10.off_ref
  2.0 0.0 copy-start
  2.0 1.4 %copy-done = f32[2,512,384]{2,1,0:T(8,128)S(1)} copy-done((f32[2,512,384]{2,1,0:T(8,128)S(1)}, f32[2,512,384]{2,1,0:T(8,128)}, u32[]{:S(2)}) %copy-start) | copy-done | bytes 1572888
  3.5 0.0 copy-start.4
  3.5 1.2 %copy-done.4 = f32[2,2,256,256]{3,2,1,0:T(8,128)S(1)} copy-done((f32[2,2,256,256]{3,2,1,0:T(8,128)S(1)}, f32[2,2,256,256]{3,2,1,0:T(8,128)}, u32[]{:S(2)}) %copy-start.4) | copy-done | bytes 1048600
  4.7 0.0 copy-start.1
  4.7 0.0 copy-start.5
  4.7 20.3 %halo.1 = (f32[2,768,640]{2,1,0:T(8,128)S(1)}, f32[2,4,256,256]{3,2,1,0:T(8,128)S(1)}) custom-call(f32[2,512,384]{2,1,0:T(8,128)S(1)} %copy-done, f32[2,2,256,256]{3,2,1,0:T(8,128)S(1)} %copy-done.4), custom_call_target="tpu_custom_call" | custom-call | bytes 67108864 | tf_op jit(solution)/shard_map/halo/pallas_call | solution.py:351
  25.0 0.0 copy-done.1
  25.0 0.0 copy-done.5
  25.0 0.0 copy-start.2
  25.0 1.4 %copy-done.2 = bf16[4,256,768]{2,1,0:T(8,128)(2,1)S(1)} copy-done((bf16[4,256,768]{2,1,0:T(8,128)(2,1)S(1)}, bf16[4,256,768]{2,1,0:T(8,128)(2,1)}, u32[]{:S(2)}) %copy-start.2) | copy-done | bytes 1572888
  26.4 0.0 copy-start.3
  26.4 1.4 %copy-done.3 = bf16[4,768,256]{2,1,0:T(8,128)(2,1)S(1)} copy-done((bf16[4,768,256]{2,1,0:T(8,128)(2,1)S(1)}, bf16[4,768,256]{2,1,0:T(8,128)(2,1)}, u32[]{:S(2)}) %copy-start.3) | copy-done | bytes 1572888
  27.8 7.7 %solve.1 = (f32[2,768,640]{2,1,0:T(8,128)S(1)}, f32[2,4,256,256]{3,2,1,0:T(8,128)S(1)}) custom-call(s32[6,2]{1,0:T(8,128)S(1)} %copy.10.off_ref, s32[1]{0:T(128)} %bitcast.5.cnt_ref, s32[1]{0:T(128)} %bitcast.2.core_ref, f32[2,768,640]{2,1,0:T(8,128)S(1)} %get-tuple-element.8.ext_ref, f32[2,4,256,256]{3,2,1,0:T(8,128)S(1)} %get-tuple-element.9.probe_ref, ...), custom_call_target="tpu_custom_call" | custom-call | tf_op jit(solution)/shard_map/solve/pallas_call | solution.py:364
  35.5 59.5 %reduce.1 = (f32[2,256,384]{2,1,0:T(8,128)S(1)}, f32[1024,256]{1,0:T(8,128)S(1)}) custom-call(f32[2,768,640]{2,1,0:T(8,128)S(1)} %get-tuple-element.10.grad, f32[2,4,256,256]{3,2,1,0:T(8,128)S(1)} %get-tuple-element.11.pg), custom_call_target="tpu_custom_call" | custom-call | tf_op jit(solution)/shard_map/reduce/pallas_call | solution.py:378
  95.0 0.9 copy.14
  95.8 1.0 %copy.15 = f32[2,2,256,256]{3,2,1,0:T(8,128)} copy(f32[2,2,256,256]{3,2,1,0:T(8,128)S(1)} %bitcast.7) | data formatting | bytes 2097152
Async XLA Ops:
  2.0 1.4 %copy-start = (f32[2,512,384]{2,1,0:T(8,128)S(1)}, f32[2,512,384]{2,1,0:T(8,128)}, u32[]{:S(2)}) copy-start(f32[2,512,384]{2,1,0:T(8,128)} %obj.1) | copy-start | bytes 4718596
  3.5 1.2 %copy-start.4 = (f32[2,2,256,256]{3,2,1,0:T(8,128)S(1)}, f32[2,2,256,256]{3,2,1,0:T(8,128)}, u32[]{:S(2)}) copy-start(f32[2,2,256,256]{3,2,1,0:T(8,128)} %probe.1) | copy-start | bytes 3145732
  4.7 20.3 %copy-start.1 = (f32[1,1,6,256,256]{4,3,2,1,0:T(8,128)S(1)}, f32[1,1,6,256,256]{4,3,2,1,0:T(8,128)}, u32[]{:S(2)}) copy-start(f32[1,1,6,256,256]{4,3,2,1,0:T(8,128)} %param.12) | copy-start | bytes 4718596
  4.7 20.3 %copy-start.5 = (bf16[2,256,256]{2,1,0:T(8,128)(2,1)S(1)}, bf16[2,256,256]{2,1,0:T(8,128)(2,1)}, u32[]{:S(2)}) copy-start(bf16[2,256,256]{2,1,0:T(8,128)(2,1)} %constant.12.clone.pick_ref) | copy-start | bytes 786436
  25.0 1.4 %copy-start.2 = (bf16[4,256,768]{2,1,0:T(8,128)(2,1)S(1)}, bf16[4,256,768]{2,1,0:T(8,128)(2,1)}, u32[]{:S(2)}) copy-start(bf16[4,256,768]{2,1,0:T(8,128)(2,1)} %constant.11.clone.wide_ref) | copy-start | bytes 4718596
  26.4 1.4 %copy-start.3 = (bf16[4,768,256]{2,1,0:T(8,128)(2,1)S(1)}, bf16[4,768,256]{2,1,0:T(8,128)(2,1)}, u32[]{:S(2)}) copy-start(bf16[4,768,256]{2,1,0:T(8,128)(2,1)} %constant.10.clone.tall_ref) | copy-start | bytes 4718596

commit v3 on v2

--- a/solution.py
+++ b/solution.py
@@ -12,6 +12,7 @@
 F32 = jnp.float32
 BF16 = jnp.bfloat16
 MESH = pl.DeviceIdType.MESH
+ANY = pl.BlockSpec(memory_space=pltpu.HBM)
 SM = pl.BlockSpec(memory_space=pltpu.SMEM)
 VM = pl.BlockSpec(memory_space=pltpu.VMEM)
 
@@ -55,12 +56,18 @@
     return jnp.dot(table, jnp.concatenate([high, low, high], 0), preferred_element_type=F32)
 
 
-def solve_kernel(off_ref, cnt_ref, core_ref, ext_ref, probe_ref, amp_ref, tall_ref, wide_ref, pick_ref,
-                 grad_ref, pg_ref, far_e, far_o):
+def solve_kernel(off_ref, cnt_ref, core_ref, ext_ref, probe_ref, amp_ref, tall_hbm, wide_hbm, pick_ref,
+                 grad_ref, pg_ref, far_e, far_o, tall_ref, wide_ref, sem):
     modes, side = probe_ref.shape[1], probe_ref.shape[2]
     half = side // 2
+    fetches = [pltpu.make_async_copy(tall_hbm, tall_ref, sem.at[0]),
+               pltpu.make_async_copy(wide_hbm, wide_ref, sem.at[1])]
+    for c in fetches:
+        c.start()
     grad_ref[...] = jnp.zeros_like(grad_ref)
     pg_ref[...] = jnp.zeros_like(pg_ref)
+    for c in fetches:
+        c.wait()
 
     @pl.loop(0, (cnt_ref[0] + 1 - core_ref[0]) // 2)
     def _(step):
@@ -365,9 +372,10 @@
         solve_kernel,
         name="solve",
         out_shape=(jax.ShapeDtypeStruct(ext.shape, F32), jax.ShapeDtypeStruct(full.shape, F32)),
-        in_specs=[SM, SM, SM] + [VM] * 6,
+        in_specs=[SM, SM, SM, VM, VM, VM, ANY, ANY, VM],
         out_specs=(VM, VM),
-        scratch_shapes=[pltpu.VMEM((modes, side, side), F32), pltpu.VMEM((modes, side, side), F32)],
+        scratch_shapes=[pltpu.VMEM((modes, side, side), F32), pltpu.VMEM((modes, side, side), F32),
+                        pltpu.VMEM(tall.shape, BF16), pltpu.VMEM(wide.shape, BF16), dma((2,))],
         compiler_params=pltpu.CompilerParams(vmem_limit_bytes=24 << 20),
     )(offsets[0, 0], counts[0], core, ext, full, amplitude[0, 0],
       jnp.asarray(tall), jnp.asarray(wide), jnp.asarray(picks))

time: 97 us -> 95.7 us (0.987)
    pallas_call x1, Pallas kernels: 59.5 us -> 46.1 us  [local(): pl.pallas_call(functools.partial(reduce_kernel, nx, ny), name='reduce', o...]
    pallas_call x1, Pallas kernels: 7.67 us -> 20.2 us  [local(): pl.pallas_call(solve_kernel, name='solve', out_shape=(jax.ShapeDtypeStruc...]
where the time goes in v3:
time: 95.7 us; the launch traced here: 96 us
  Pallas kernels  86.6 us (90%)
  local copies, waits for them, and re-layouts  8.07 us (8%)
  between operations  1.33 us (1%)
    pallas_call x1, Pallas kernels, local(): pl.pallas_call(functools.partial(reduce_kernel, nx, ny), name='reduce', o...  46.1 us
    pallas_call x1, Pallas kernels, local(): pl.pallas_call(functools.partial(halo_kernel, nx, ny), name='halo', out_s...  20.3 us
    pallas_call x1, Pallas kernels, local(): pl.pallas_call(solve_kernel, name='solve', out_shape=(jax.ShapeDtypeStruc...  20.2 us
    unnamed x14, local copies, waits for them, and re-layouts  7.3 us

profile of v3, /device:TPU:0, one launch (start us, length us, event | category | flops | bytes accessed | tf_op | source)
XLA Modules:
  0.0 96.0 jit_solution(13915439198872908416)
XLA Ops:
  1.3 0.8 copy.10.off_ref
  2.0 0.0 copy-start
  2.0 1.4 %copy-done = f32[2,512,384]{2,1,0:T(8,128)S(1)} copy-done((f32[2,512,384]{2,1,0:T(8,128)S(1)}, f32[2,512,384]{2,1,0:T(8,128)}, u32[]{:S(2)}) %copy-start) | copy-done | bytes 1572888
  3.5 0.0 copy-start.4
  3.5 1.2 %copy-done.4 = f32[2,2,256,256]{3,2,1,0:T(8,128)S(1)} copy-done((f32[2,2,256,256]{3,2,1,0:T(8,128)S(1)}, f32[2,2,256,256]{3,2,1,0:T(8,128)}, u32[]{:S(2)}) %copy-start.4) | copy-done | bytes 1048600
  4.7 0.0 copy-start.1
  4.7 0.0 copy-start.5
  4.7 20.3 %halo.1 = (f32[2,768,640]{2,1,0:T(8,128)S(1)}, f32[2,4,256,256]{3,2,1,0:T(8,128)S(1)}) custom-call(f32[2,512,384]{2,1,0:T(8,128)S(1)} %copy-done, f32[2,2,256,256]{3,2,1,0:T(8,128)S(1)} %copy-done.4), custom_call_target="tpu_custom_call" | custom-call | bytes 67108864 | tf_op jit(solution)/shard_map/halo/pallas_call | solution.py:358
  25.0 0.0 copy-done.1
  25.0 0.0 copy-done.5
  25.0 0.0 copy-start.2
  25.0 1.4 %copy-done.2 = bf16[4,256,768]{2,1,0:T(8,128)(2,1)S(1)} copy-done((bf16[4,256,768]{2,1,0:T(8,128)(2,1)S(1)}, bf16[4,256,768]{2,1,0:T(8,128)(2,1)}, u32[]{:S(2)}) %copy-start.2) | copy-done | bytes 1572888
  26.4 0.0 copy-start.3
  26.4 1.4 %copy-done.3 = bf16[4,768,256]{2,1,0:T(8,128)(2,1)S(1)} copy-done((bf16[4,768,256]{2,1,0:T(8,128)(2,1)S(1)}, bf16[4,768,256]{2,1,0:T(8,128)(2,1)}, u32[]{:S(2)}) %copy-start.3) | copy-done | bytes 1572888
  27.8 20.2 %solve.1 = (f32[2,768,640]{2,1,0:T(8,128)S(1)}, f32[2,4,256,256]{3,2,1,0:T(8,128)S(1)}) custom-call(s32[6,2]{1,0:T(8,128)S(1)} %copy.10.off_ref, s32[1]{0:T(128)} %bitcast.5.cnt_ref, s32[1]{0:T(128)} %bitcast.2.core_ref, f32[2,768,640]{2,1,0:T(8,128)S(1)} %get-tuple-element.8.ext_ref, f32[2,4,256,256]{3,2,1,0:T(8,128)S(1)} %get-tuple-element.9.probe_ref, ...), custom_call_target="tpu_custom_call" | custom-call | tf_op jit(solution)/shard_map/solve/pallas_call | solution.py:371
  48.0 46.1 %reduce.1 = (f32[2,256,384]{2,1,0:T(8,128)S(1)}, f32[1024,256]{1,0:T(8,128)S(1)}) custom-call(f32[2,768,640]{2,1,0:T(8,128)S(1)} %get-tuple-element.10.grad, f32[2,4,256,256]{3,2,1,0:T(8,128)S(1)} %get-tuple-element.11.pg), custom_call_target="tpu_custom_call" | custom-call | tf_op jit(solution)/shard_map/reduce/pallas_call | solution.py:386
  94.2 0.9 copy.14
  95.1 1.0 %copy.15 = f32[2,2,256,256]{3,2,1,0:T(8,128)} copy(f32[2,2,256,256]{3,2,1,0:T(8,128)S(1)} %bitcast.7) | data formatting | bytes 2097152
Async XLA Ops:
  2.0 1.4 %copy-start = (f32[2,512,384]{2,1,0:T(8,128)S(1)}, f32[2,512,384]{2,1,0:T(8,128)}, u32[]{:S(2)}) copy-start(f32[2,512,384]{2,1,0:T(8,128)} %obj.1) | copy-start | bytes 4718596
  3.5 1.2 %copy-start.4 = (f32[2,2,256,256]{3,2,1,0:T(8,128)S(1)}, f32[2,2,256,256]{3,2,1,0:T(8,128)}, u32[]{:S(2)}) copy-start(f32[2,2,256,256]{3,2,1,0:T(8,128)} %probe.1) | copy-start | bytes 3145732
  4.7 20.3 %copy-start.1 = (f32[1,1,6,256,256]{4,3,2,1,0:T(8,128)S(1)}, f32[1,1,6,256,256]{4,3,2,1,0:T(8,128)}, u32[]{:S(2)}) copy-start(f32[1,1,6,256,256]{4,3,2,1,0:T(8,128)} %param.12) | copy-start | bytes 4718596
  4.7 20.3 %copy-start.5 = (bf16[2,256,256]{2,1,0:T(8,128)(2,1)S(1)}, bf16[2,256,256]{2,1,0:T(8,128)(2,1)}, u32[]{:S(2)}) copy-start(bf16[2,256,256]{2,1,0:T(8,128)(2,1)} %constant.12.clone.pick_ref) | copy-start | bytes 786436
  25.0 1.4 %copy-start.2 = (bf16[4,256,768]{2,1,0:T(8,128)(2,1)S(1)}, bf16[4,256,768]{2,1,0:T(8,128)(2,1)}, u32[]{:S(2)}) copy-start(bf16[4,256,768]{2,1,0:T(8,128)(2,1)} %constant.11.clone.wide_hbm) | copy-start | bytes 4718596
  26.4 1.4 %copy-start.3 = (bf16[4,768,256]{2,1,0:T(8,128)(2,1)S(1)}, bf16[4,768,256]{2,1,0:T(8,128)(2,1)}, u32[]{:S(2)}) copy-start(bf16[4,768,256]{2,1,0:T(8,128)(2,1)} %constant.10.clone.tall_hbm) | copy-start | bytes 4718596
